TPU v7x, 512 devices: a whole 4x4x16 slice. The times are simulated.
512 devices in a mesh: dp: 8 (over z_lo), mp: 64 (over x, z_hi, y, core).
Axes of the slice: x: 4, y: 4, z: 16 (z_hi: 2, z_lo: 8; z = z_hi * 8 + z_lo), core: 2. Of those that a mesh axis runs over, the one named last changes fastest.
Arguments:
- base_rows: bfloat16 [1024, 8192], P('dp', 'mp'), may hold values from -6 to 6
- layer_rows: bfloat16 [1024, 8192], P('dp', 'mp'), may hold values from -6 to 6
- cross_weight: bfloat16 [8192, 8192], P(None, 'mp'), may hold values from -0.0625 to 0.0625
- cross_bias: float32 [8192], P('mp'), may hold values from -3 to 3
- upstream: bfloat16 [1024, 8192], P('dp', 'mp'), may hold values from -6 to 6
Outputs:
- crossed: bfloat16 [1024, 8192], P('dp', 'mp')
- grad_base: bfloat16 [1024, 8192], P('dp', 'mp')
- grad_layer: bfloat16 [1024, 8192], P('dp', 'mp')
- grad_weight: float32 [8192, 8192], P('dp', 'mp')
- grad_bias: float32 [8192], P('mp')
All inputs are finite; a program needn't handle non-finite values.
Results may differ from a plain program's by a relative error of at most 0.0041.
Values may be sent and summed in bfloat16 or wider, within the bound.
A program may use at most 64 MiB of HBM per device.

v0:
```python
import jax
import jax.numpy as jnp
from jax import lax
from jax.sharding import Mesh
from jax.sharding import PartitionSpec as P

MP = ("mp_0", "mp_1", "mp_2", "mp_3")


def joined_along(parts, dim):
    shape = list(parts.shape[1:])
    shape[dim] *= parts.shape[0]
    return jnp.moveaxis(parts, 0, dim).reshape(shape)


def sent_to_all(value, axis):
    size = lax.axis_size(axis)
    return lax.all_to_all(
        jnp.broadcast_to(value[None], (size, *value.shape)), axis, 0, 0, tiled=True
    )


def collect(value, axis, dim):
    return joined_along(sent_to_all(value, axis), dim)


def gather_axes(value, axes, dim):
    far, near = axes
    parts = sent_to_all(sent_to_all(value, far), near)
    return joined_along(parts.swapaxes(0, 1).reshape(-1, *value.shape), dim)


def over_copies(value, axis):
    return sent_to_all(value, axis).sum(axis=0)


def local(base_rows, layer_rows, cross_weight, cross_bias, upstream):
    width = cross_weight.shape[1]
    total = cross_weight.shape[0]
    groups = lax.axis_size("dp")
    share = width // groups
    own_cols = lax.dynamic_slice_in_dim(cross_weight, lax.axis_index("dp") * share, share, 1)
    pieces = lax.all_to_all(own_cols, MP, split_axis=0, concat_axis=1, tiled=True)
    joined = collect(pieces, "dp", 1)
    panels = total // width
    joined = joined.reshape(width, groups, panels, share)
    row_block = jnp.transpose(joined, (0, 2, 1, 3)).reshape(width, total)
    full_rows = gather_axes(layer_rows, (("mp_0", "mp_1", "mp_2"), "mp_3"), 1)
    mixed = jnp.dot(full_rows, cross_weight, preferred_element_type=jnp.float32) + cross_bias
    base = base_rows.astype(jnp.float32)
    crossed = (base * mixed + layer_rows.astype(jnp.float32)).astype(jnp.bfloat16)
    upper = upstream.astype(jnp.float32)
    delta = upper * base
    delta_low = delta.astype(jnp.bfloat16)
    grad_base = (upper * mixed).astype(jnp.bfloat16)
    back = lax.dot_general(
        lax.all_gather(delta_low, MP, axis=1, tiled=True),
        row_block,
        (((1,), (1,)), ((), ())),
        preferred_element_type=jnp.float32,
    )
    grad_layer = (upper + back).astype(jnp.bfloat16)
    scale = jnp.float32(base_rows.shape[0] * groups) ** (-0.5)
    grad_weight = (
        lax.psum_scatter(
            lax.dot_general(
                full_rows, delta_low, (((0,), (0,)), ((), ())), preferred_element_type=jnp.float32
            ),
            "dp",
            scatter_dimension=0,
            tiled=True,
        )
        * scale
    )
    grad_bias = over_copies(jnp.sum(delta, axis=0), "dp") * scale
    return (crossed, grad_base, grad_layer, grad_weight, grad_bias)


def solution(mesh):
    finer = Mesh(
        mesh.devices.reshape(mesh.shape["dp"], 4, 2, 4, 2), ("dp", "mp_0", "mp_1", "mp_2", "mp_3")
    )
    return jax.shard_map(
        local,
        mesh=finer,
        in_specs=(P("dp", MP), P("dp", MP), P(None, MP), P(MP), P("dp", MP)),
        out_specs=(P("dp", MP), P("dp", MP), P("dp", MP), P("dp", MP), P(MP)),
        check_vma=False,
    )
```

profile of v0, /device:TPU:1, one launch (start us, length us, event | category | flops | bytes accessed | tf_op | source)
XLA Modules:
  0.0 344.3 jit_solution(5765860390326713787)
XLA Ops:
  8.0 0.0 copy-start
  8.0 0.0 all-gather.2.cloned.1.call-start
  8.1 1.1 broadcast_in_dim.10
  9.2 50.3 %all_to_all.37 = bf16[32,128,128]{2,1,0:T(8,128)(2,1)S(1)} all-to-all(bf16[32,128,128]{2,1,0:T(8,128)(2,1)S(1)} %broadcast_in_dim.10), channel_id=1, replica_groups=mesh['dp'=8,'mp_0'=4,'mp_1'=2,'mp_2'=4,'mp_3'=2] {'mp_0','mp_1','mp_2'}, dimensions={0} | all-to-all | bytes 2097152 | tf_op jit(solution)/shard_map/all_to_all | solution.py:18
  59.5 0.7 broadcast_in_dim.11
  60.2 7.0 %all_to_all.38 = bf16[2,32,128,128]{3,2,1,0:T(8,128)(2,1)S(1)} all-to-all(bf16[2,32,128,128]{3,2,1,0:T(8,128)(2,1)S(1)} %broadcast_in_dim.11), channel_id=1, replica_groups=mesh['dp'=8,'mp_0'=4,'mp_1'=2,'mp_2'=4,'mp_3'=2] {'mp_3'}, dimensions={0} | all-to-all | bytes 4194304 | tf_op jit(solution)/shard_map/all_to_all | solution.py:18
  67.2 1.5 copy.31
  68.7 0.0 copy-start.2
  68.7 0.0 copy-start.3
  68.7 0.0 copy-start.4
  68.7 0.0 copy-start.5
  68.7 4.2 %copy.32 = bf16[128,64,128]{0,2,1:T(8,128)(2,1)} copy(bf16[128,64,128]{2,0,1:T(8,128)(2,1)} %bitcast.28) | data formatting | bytes 4194304 | tf_op jit(solution)/shard_map/transpose | solution.py:13
  72.9 0.0 copy-done
  72.9 0.0 copy-done.2
  72.9 0.0 copy-done.3
  72.9 0.0 copy-done.4
  72.9 0.0 copy-done.5
  72.9 3.0 fusion.3
  75.9 0.0 all-gather.2.cloned.1.call-update
  75.9 2.0 constant_dynamic-slice_fusion
  77.9 0.0 copy-start.1
  77.9 2.5 copy.34
  80.4 5.4 %all-to-all-start.2 = ((bf16[64,128,16]{1,2,0:T(8,128)(2,1)}), bf16[64,128,16]{1,2,0:T(8,128)(2,1)S(1)}, u32[]{:S(2)}, u32[]{:S(2)}) async-start(bf16[64,128,16]{1,2,0:T(8,128)(2,1)} %copy.34), calls=%async_computation.2 | async-start | bytes 524288 | tf_op jit(solution)/shard_map/all_to_all | solution.py:43
  85.8 0.0 reduce-scatter.2.cloned.1.call-start
  85.8 0.0 copy-done.1
  85.9 4.3 %convolution_bitcast_fusion = f32[8192,128]{0,1:T(8,128)} fusion(bf16[128,128]{1,0:T(8,128)(2,1)S(1)} %copy-done.1, bf16[128,8192]{0,1:T(8,128)(2,1)} %bitcast.26), kind=kOutput, calls=%fused_computation | convolution fusion | flops 268435456 | bytes 6324224 | tf_op jit(solution)/shard_map/dot_general | solution.py:66
  90.1 0.0 reduce-scatter.2.cloned.1.call-update
  90.1 14.2 %all-to-all-done.2 = bf16[64,128,16]{1,2,0:T(8,128)(2,1)S(1)} async-done(((bf16[64,128,16]{1,2,0:T(8,128)(2,1)}), bf16[64,128,16]{1,2,0:T(8,128)(2,1)S(1)}, u32[]{:S(2)}, u32[]{:S(2)}) %all-to-all-start.2) | async-done | bytes 262176 | tf_op jit(solution)/shard_map/all_to_all | solution.py:43
  104.3 42.3 %all_to_all.39 = f32[8,1,128]{2,1,0:T(1,128)S(1)} all-to-all(f32[8,1,128]{2,1,0:T(1,128)S(1)} %broadcast_in_dim.14), channel_id=1, replica_groups=mesh['dp'=8,'mp_0'=4,'mp_1'=2,'mp_2'=4,'mp_3'=2] {'dp'}, dimensions={0} | all-to-all | bytes 8192 | tf_op jit(solution)/shard_map/all_to_all | solution.py:18
  146.6 1.6 broadcast_in_dim.13
  148.3 4.3 %all-to-all-start.3 = ((bf16[8,128,1024]{1,2,0:T(8,128)(2,1)}), bf16[8,128,1024]{1,2,0:T(8,128)(2,1)}, u32[]{:S(2)}, u32[]{:S(2)}) async-start(bf16[8,128,1024]{1,2,0:T(8,128)(2,1)} %broadcast_in_dim.13), calls=%async_computation.3 | async-start | bytes 4194304 | tf_op jit(solution)/shard_map/all_to_all | solution.py:18
  152.7 0.5 broadcast_multiply_fusion.1
  153.2 174.5 %all-to-all-done.3 = bf16[8,128,1024]{1,2,0:T(8,128)(2,1)} async-done(((bf16[8,128,1024]{1,2,0:T(8,128)(2,1)}), bf16[8,128,1024]{1,2,0:T(8,128)(2,1)}, u32[]{:S(2)}, u32[]{:S(2)}) %all-to-all-start.3) | async-done | bytes 2097184 | tf_op jit(solution)/shard_map/all_to_all | solution.py:18
  327.6 3.6 %copy.35 = bf16[128,64,8,16]{0,3,2,1:T(8,128)(2,1)} copy(bf16[128,64,8,16]{0,3,1,2:T(8,128)(2,1)} %bitcast.9) | data formatting | bytes 4194304 | tf_op jit(solution)/shard_map/transpose | solution.py:47
  331.2 0.0 all-gather.2.cloned.1.call-done
  331.2 3.5 %fusion = bf16[128,128]{1,0:T(8,128)(2,1)} fusion(bf16[128,8192]{1,0:T(8,128)(2,1)} %all-gather.2.cloned.1.call-done, bf16[128,8192]{0,1:T(8,128)(2,1)} %bitcast.27, bf16[128,128]{1,0:T(8,128)(2,1)S(1)} %copy-done.2), kind=kOutput, calls=%fused_computation.3 | convolution fusion | flops 268484608 | bytes 4259840 | tf_op jit(solution)/shard_map/dot_general | solution.py:56
  334.7 0.0 reduce-scatter.2.cloned.1.call-done
  334.7 1.1 broadcast_multiply_fusion
  335.8 1.0 copy.37
  (2 shorter events, 0.0 us)
Async XLA Ops:
  8.0 64.9 %copy-start = (bf16[8192,128]{1,0:T(8,128)(2,1)S(1)}, bf16[8192,128]{1,0:T(8,128)(2,1)}, u32[]{:S(2)}) copy-start(bf16[8192,128]{1,0:T(8,128)(2,1)} %param.7) | copy-start | bytes 6291460
  8.0 323.2 %all-gather.2.cloned.1.call-start = ((), (), s32[]{:S(2)}) async-start(), calls=%async_computation.6 | async-start | bytes 2129920 | tf_op jit(solution)/shard_map/all_gather | solution.py:57
  68.7 4.2 %copy-start.2 = (bf16[128,128]{1,0:T(8,128)(2,1)S(1)}, bf16[128,128]{1,0:T(8,128)(2,1)}, u32[]{:S(2)}) copy-start(bf16[128,128]{1,0:T(8,128)(2,1)} %param.9) | copy-start | bytes 98308
  68.7 4.2 %copy-start.3 = (bf16[128,128]{1,0:T(8,128)(2,1)S(1)}, bf16[128,128]{1,0:T(8,128)(2,1)}, u32[]{:S(2)}) copy-start(bf16[128,128]{1,0:T(8,128)(2,1)} %param.6) | copy-start | bytes 98308
  68.7 4.2 %copy-start.4 = (bf16[128,128]{1,0:T(8,128)(2,1)S(1)}, bf16[128,128]{1,0:T(8,128)(2,1)}, u32[]{:S(2)}) copy-start(bf16[128,128]{1,0:T(8,128)(2,1)} %param.5) | copy-start | bytes 98308
  68.7 4.2 %copy-start.5 = (f32[128]{0:T(128)S(1)}, f32[128]{0:T(128)}, u32[]{:S(2)}) copy-start(f32[128]{0:T(128)} %param.8) | copy-start | bytes 1540
  77.9 8.0 %copy-start.1 = (bf16[128,128]{1,0:T(8,128)(2,1)S(1)}, bf16[128,128]{1,0:T(8,128)(2,1)}, u32[]{:S(2)}) copy-start(bf16[128,128]{1,0:T(8,128)(2,1)} %get-tuple-element.39) | copy-start | bytes 98308
  80.4 23.9 %all-to-all-start.2 = ((bf16[64,128,16]{1,2,0:T(8,128)(2,1)}), bf16[64,128,16]{1,2,0:T(8,128)(2,1)S(1)}, u32[]{:S(2)}, u32[]{:S(2)}) async-start(bf16[64,128,16]{1,2,0:T(8,128)(2,1)} %copy.34), calls=%async_computation.2 | async-start | bytes 524288 | tf_op jit(solution)/shard_map/all_to_all | solution.py:43
  85.8 248.9 %reduce-scatter.2.cloned.1.call-start = ((), (), s32[]{:S(2)}) async-start(), calls=%async_computation.7 | async-start | bytes 4718592 | tf_op jit(solution)/shard_map/reduce_scatter | solution.py:65
  148.3 179.3 %all-to-all-start.3 = ((bf16[8,128,1024]{1,2,0:T(8,128)(2,1)}), bf16[8,128,1024]{1,2,0:T(8,128)(2,1)}, u32[]{:S(2)}, u32[]{:S(2)}) async-start(bf16[8,128,1024]{1,2,0:T(8,128)(2,1)} %broadcast_in_dim.13), calls=%async_computation.3 | async-start | bytes 4194304 | tf_op jit(solution)/shard_map/all_to_all | solution.py:18
Sparse Core Ops, SparseCore 0:
  76.0 183.0 all-gather.1
Sparse Core Ops, SparseCore 1:
  90.2 240.2 reduce-scatter.1
where the time goes:
time: 345 us; the launch traced here: 344 us
  waiting for transfers between devices  189 us (55%)
  blocking collectives  99.6 us (29%)
  local copies, waits for them, and re-layouts  18.2 us (5%)
  between operations  15.6 us (5%)
  matrix products  10.8 us (3%)
  starting transfers between devices  9.81 us (3%)
    all_to_all x1, waiting for transfers between devices, sent_to_all(): lax.all_to_all(jnp.broadcast_to(value[None], (size, *value.shape)), axis,...  174 us
    all_to_all x3, blocking collectives, sent_to_all(): lax.all_to_all(jnp.broadcast_to(value[None], (size, *value.shape)), axis,...  99.6 us
    all_to_all x1, waiting for transfers between devices, local(): lax.all_to_all(own_cols, MP, split_axis=0, concat_axis=1, tiled=True)  14.2 us
  transfers between devices with their start and end apart: 4, of which 2 were waited for; matrix products, arithmetic and copies ran while one was open for 5% of the time, Pallas kernels for 0%

commit v1 on v0

v1 whole, which is shorter than its diff:
```python
import functools

import jax
import jax.numpy as jnp
from jax import lax
from jax.experimental import pallas as pl
from jax.experimental.pallas import tpu as pltpu
from jax.sharding import PartitionSpec as P

MESH = pl.DeviceIdType.MESH
F32 = jnp.float32
BF16 = jnp.bfloat16
N_SEMS = 128


def kernel(
    scale,
    base,
    lay,
    up,
    bias,
    w4,
    crossed,
    gbase,
    glayer,
    gw,
    gbias,
    wo,
    wp,
    dl,
    dlp,
    xa,
    fs,
    xb,
    do,
    dp_,
    bs,
    part,
    r1lo,
    r1hi,
    rl,
    rr,
    s1,
    b2,
    r2,
    tt,
    zs,
    zr,
    mixp,
    mixr,
    gws,
    send,
    recv,
    lsem,
):
    d = lax.axis_index("dp")
    m = lax.axis_index("mp")
    c = lax.rem(m, 2)
    y = lax.rem(lax.div(m, 2), 4)
    h = lax.rem(lax.div(m, 8), 2)
    x = lax.div(m, 16)
    oh = 1 - h
    oc = 1 - c

    def dev(x_=None, y_=None, h_=None, c_=None, d_=None):
        x_ = x if x_ is None else x_
        y_ = y if y_ is None else y_
        h_ = h if h_ is None else h_
        c_ = c if c_ is None else c_
        d_ = d if d_ is None else d_
        return (d_, ((x_ * 2 + h_) * 4 + y_) * 2 + c_)

    def plus(v, k):
        return lax.rem(v + k, 4)

    ids = iter(range(N_SEMS))
    sent = []

    def put(src, dst, to, k=None):
        k = next(ids) if k is None else k
        copy = pltpu.make_async_remote_copy(
            src_ref=src,
            dst_ref=dst,
            send_sem=send.at[k],
            recv_sem=recv.at[k],
            device_id=to,
            device_id_type=MESH,
        )
        copy.start()
        sent.append(copy)
        return k

    def got(k, landed):
        pltpu.make_async_remote_copy(
            src_ref=landed,
            dst_ref=landed,
            send_sem=send.at[k],
            recv_sem=recv.at[k],
            device_id=dev(c_=oc),
            device_id_type=MESH,
        ).wait_recv()

    load_w = pltpu.make_async_copy(w4.at[:, c], wo, lsem.at[0])
    load_w.start()
    own_x = pltpu.make_async_copy(lay, xa.at[h, x, y], lsem.at[1])
    own_x.start()

    barrier = pltpu.get_barrier_semaphore()
    near = [dev(c_=oc)]
    near += [dev(x_=plus(x, k)) for k in (1, 2, 3)]
    near += [dev(y_=plus(y, k)) for k in (1, 2, 3)]
    z = h * 8 + d
    for k in range(1, 16):
        zk = lax.rem(z + k, 16)
        near.append(dev(h_=lax.div(zk, 8), d_=lax.rem(zk, 8)))
    for to in near:
        pl.semaphore_signal(barrier, inc=1, device_id=to, device_id_type=MESH)

    upper = up[...].astype(F32)
    basef = base[...].astype(F32)
    delta = upper * basef
    low = delta.astype(BF16).reshape(4, 32, 128)
    dl[...] = low
    do[:, d] = low
    bs[d] = jnp.broadcast_to(jnp.sum(delta, axis=0, keepdims=True), (8, 128))

    own_x.wait()
    pl.semaphore_wait(barrier, len(near))

    k_dlp = put(dl, dlp, dev(c_=oc))
    k_wp = [
        put(w4.at[pl.ds(8 * j, 8), oc], wp.at[pl.ds(8 * j, 8)], dev(c_=oc))
        for j in range(4)
    ]
    k_zx = put(lay, xa.at[h, x, y], dev(h_=oh))

    def ag1(view, n):
        half = n // 2
        ks = []
        for j in (1, 3, 2):
            a = view(x, y, 0, half)
            b = view(x, y, half, half)
            ka = put(a, a, dev(x_=plus(x, j)))
            kb = put(b, b, dev(y_=plus(y, j)))
            ks.append((j, ka, kb))
        return ks

    def ag1_wait(view, n, ks):
        half = n // 2
        for j, ka, kb in ks:
            got(ka, view(plus(x, 4 - j), y, 0, half))
            got(kb, view(x, plus(y, 4 - j), half, half))

    every = pl.ds(0, 4)

    def ag2(view, n):
        half = n // 2
        ks = []
        for j in (1, 3):
            a = view(every, y, 0, half)
            b = view(x, every, half, half)
            ks.append((put(a, a, dev(y_=plus(y, j))), put(b, b, dev(x_=plus(x, j)))))
        return ks

    def ag2_forward(view, n, ks):
        half = n // 2
        out = []
        for (ka, kb), j, part_of in zip(ks, (1, 3), (pl.ds(0, 2), pl.ds(2, 2)), strict=True):
            ys, xs = plus(y, 4 - j), plus(x, 4 - j)
            got(ka, view(every, ys, 0, half))
            a = view(part_of, ys, 0, half)
            fa = put(a, a, dev(y_=plus(y, j)))
            got(kb, view(xs, every, half, half))
            b = view(xs, part_of, half, half)
            fb = put(b, b, dev(x_=plus(x, j)))
            out.append((fa, fb, part_of))
        return out

    def ag2_wait(view, n, ks):
        half = n // 2
        for fa, fb, part_of in ks:
            got(fa, view(part_of, plus(y, 2), 0, half))
            got(fb, view(plus(x, 2), part_of, half, half))

    def x_own(xs, ys, q, nq):
        return xa.at[h, xs, ys, pl.ds(q, nq)]

    def x_other(xs, ys, q, nq):
        return xa.at[oh, xs, ys, pl.ds(q, nq)]

    def x_block(xs, ys, q, nq):
        return xb.at[xs, ys, pl.ds(q, nq)]

    own1 = ag1(x_own, 4)

    k_fs = []
    for j in (1, 2, 3):
        t = plus(x, j)
        k_fs.append(put(lay.at[t], fs.at[x], dev(x_=t)))
    for j, k in zip((1, 2, 3), k_fs, strict=True):
        got(k, fs.at[plus(x, 4 - j)])
    z_first = [next(ids) for _ in range(8)]
    z_recv = z_first[0]
    z_sent = []
    for j in range(4):
        for hh in (0, 1):
            s = plus(x, j)
            src = lay.at[x] if j == 0 else fs.at[s]
            d_to = 2 * s + h
            mine = jnp.logical_and(h == hh, d_to == d)
            dst = xb.at[x, y, d]
            copy = pltpu.make_async_remote_copy(
                src_ref=src,
                dst_ref=dst,
                send_sem=send.at[z_first[2 * j + hh]],
                recv_sem=recv.at[z_recv + d],
                device_id=dev(h_=hh, d_=d_to),
                device_id_type=MESH,
            )
            stay = pltpu.make_async_copy(src, dst, recv.at[z_recv + d])

            @pl.when(mine)
            def _(stay=stay):
                stay.start()

            @pl.when(jnp.logical_not(mine))
            def _(copy=copy):
                copy.start()

            z_sent.append((mine, copy))

    k_do = []
    for j in range(1, 8):
        t = lax.rem(d + j, 8)
        kd = put(dl, do.at[:, d], dev(d_=t))
        kb = put(bs.at[d], bs.at[d], dev(d_=t))
        k_do.append((j, kd, kb))

    ag1_wait(x_own, 4, own1)
    own2 = ag2(x_own, 4)

    load_w.wait()
    got(k_dlp, dlp)
    d_own = dl[...].reshape(128, 128)
    d_other = dlp[...].reshape(128, 128)
    nt = (((1,), (1,)), ((), ()))
    for i in range(8):
        if i % 2 == 0:
            got(k_wp[i // 2], wp.at[pl.ds(4 * i, 8)])
        xs, hs = i // 2, i % 2
        term = lax.dot_general(
            wo[4 * i : 4 * i + 4].reshape(512, 128), d_own, nt, preferred_element_type=F32
        ) + lax.dot_general(
            wp[4 * i : 4 * i + 4].reshape(512, 128), d_other, nt, preferred_element_type=F32
        )
        term = term.astype(BF16).reshape(4, 128, 128)
        part[0, xs, :, hs] = term[:, 0:64]
        for ys in range(4):
            part[1, ys, xs, hs] = term[ys, 64:128]

    lo, hi = pl.ds(0, 2), pl.ds(2, 2)

    def to_line(half, j):
        return dev(x_=plus(x, j)) if half == 0 else dev(y_=plus(y, j))

    def to_line2(half, j):
        return dev(y_=plus(y, j)) if half == 0 else dev(x_=plus(x, j))

    k_rs = []
    for half in (0, 1):
        me = x if half == 0 else y
        a = put(part.at[half, plus(me, 2), lo], r1lo.at[half], to_line(half, 1))
        b = put(part.at[half, plus(me, 2), hi], r1hi.at[half], to_line(half, 3))
        e = put(part.at[half, plus(me, 1), hi], rl.at[half, hi], to_line(half, 1))
        f = put(part.at[half, plus(me, 3), lo], rr.at[half, lo], to_line(half, 3))
        k_rs.append((a, b, e, f))

    own3 = ag2_forward(x_own, 4, own2)

    k_rs2 = []
    for half in (0, 1):
        me = x if half == 0 else y
        a, b, _, _ = k_rs[half]
        got(a, r1lo.at[half])
        t = plus(me, 1)
        part[half, t, lo] = (part[half, t, lo].astype(F32) + r1lo[half].astype(F32)).astype(BF16)
        e = put(part.at[half, t, lo], rl.at[half, lo], to_line(half, 1))
        got(b, r1hi.at[half])
        t = plus(me, 3)
        part[half, t, hi] = (part[half, t, hi].astype(F32) + r1hi[half].astype(F32)).astype(BF16)
        f = put(part.at[half, t, hi], rr.at[half, hi], to_line(half, 3))
        k_rs2.append((e, f))

    def mixed_terms(hs, acc):
        for xs in range(4):
            rows = jnp.concatenate([xa[hs, xs, ys].reshape(128, 128) for ys in range(4)], axis=1)
            s0 = (xs * 2 + hs) * 4
            cols = jnp.concatenate(
                [
                    wo[pl.ds(s0, 4)].reshape(512, 128),
                    wp[pl.ds(s0, 4)].reshape(512, 128),
                ],
                axis=1,
            )
            acc = acc + jnp.dot(rows, cols, preferred_element_type=F32)
        return acc

    ag2_wait(x_own, 4, own3)
    acc = mixed_terms(h, jnp.zeros((128, 256), F32))
    mixp[...] = acc

    got(k_zx, xa.at[oh, x, y])
    other1 = ag1(x_other, 4)

    for s in range(8):
        got(z_recv + s, xb.at[x, y, s])
    block1 = ag1(x_block, 8)

    k_s2 = []
    for half in (0, 1):
        me, me2 = (x, y) if half == 0 else (y, x)
        got(k_rs[half][2], rl.at[half, hi])
        got(k_rs[half][3], rr.at[half, lo])
        got(k_rs2[half][0], rl.at[half, lo])
        got(k_rs2[half][1], rr.at[half, hi])
        total = part[half, me].astype(F32) + rl[half].astype(F32) + rr[half].astype(F32)
        s1[half] = total
        b2[half] = total.astype(BF16)
        ks = []
        for j in (1, 3, 2):
            t = plus(me2, j)
            ks.append((j, put(b2.at[half, t], r2.at[half, j - 1], to_line2(half, j))))
        k_s2.append(ks)

    ag1_wait(x_other, 4, other1)
    other2 = ag2(x_other, 4)
    ag1_wait(x_block, 8, block1)
    block2 = ag2(x_block, 8)

    for half in (0, 1):
        me2 = y if half == 0 else x
        for j, k in k_s2[half]:
            got(k, r2.at[half, j - 1])
        tt[half] = (
            s1[half, me2]
            + r2[half, 0].astype(F32)
            + r2[half, 1].astype(F32)
            + r2[half, 2].astype(F32)
        )
    zs[...] = tt[:, oh].astype(BF16)
    k_zr = put(zs, zr, dev(h_=oh))

    other3 = ag2_forward(x_other, 4, other2)
    block3 = ag2_forward(x_block, 8, block2)

    for j, kd, kb in k_do:
        s = lax.rem(d + 8 - j, 8)
        got(kd, do.at[:, s])
        got(kb, bs.at[s])
    k_dp = put(do, dp_, dev(c_=oc))

    ag2_wait(x_other, 4, other3)
    acc = mixed_terms(oh, mixp[...])
    mixp[...] = acc
    k_mix = put(mixp.at[:, pl.ds(128, 128)], mixr, dev(c_=oc))

    ag2_wait(x_block, 8, block3)
    got(k_dp, dp_)
    tn = (((0,), (0,)), ((), ()))
    acc = jnp.zeros((512, 256), F32)
    for xs in range(4):
        feats = jnp.concatenate([xb[xs, ys].reshape(256, 128) for ys in range(4)], axis=1)
        cols = jnp.concatenate([do[xs].reshape(256, 128), dp_[xs].reshape(256, 128)], axis=1)
        acc = acc + lax.dot_general(feats, cols, tn, preferred_element_type=F32)
    acc = acc * scale
    gws[...] = acc[:, 128:256].reshape(4, 128, 128)
    k_gw = put(gws, gw.at[:, c], dev(c_=oc))
    gw[:, c] = acc[:, 0:128].reshape(4, 128, 128)

    gbias[...] = jnp.sum(bs[:, 0], axis=0, keepdims=True) * scale

    got(k_mix, mixr)
    mixed = mixp[:, 0:128] + mixr[...] + bias[...]
    crossed[...] = (basef * mixed + lay[...].reshape(128, 128).astype(F32)).astype(BF16)
    gbase[...] = (upper * mixed).astype(BF16)

    got(k_zr, zr)
    back = (tt[:, h] + zr[...].astype(F32)).reshape(128, 128)
    glayer[...] = (upper + back.T).astype(BF16)

    got(k_gw, gw.at[:, oc])
    for copy in sent:
        copy.wait_send()
    for mine, copy in z_sent:

        @pl.when(jnp.logical_not(mine))
        def _(copy=copy):
            copy.wait_send()


def local(base_rows, layer_rows, cross_weight, cross_bias, upstream):
    vmem = pl.BlockSpec(memory_space=pltpu.VMEM)
    scale = float((base_rows.shape[0] * 8) ** -0.5)
    small = jax.ShapeDtypeStruct((128, 128), BF16)
    crossed, gbase, glayer, gw, gbias = pl.pallas_call(
        functools.partial(kernel, scale),
        out_shape=(
            small,
            small,
            small,
            jax.ShapeDtypeStruct((4, 2, 128, 128), F32),
            jax.ShapeDtypeStruct((1, 128), F32),
        ),
        in_specs=[vmem, vmem, vmem, vmem, pl.BlockSpec(memory_space=pl.ANY)],
        out_specs=(vmem, vmem, vmem, vmem, vmem),
        scratch_shapes=[
            pltpu.VMEM((32, 128, 128), BF16),
            pltpu.VMEM((32, 128, 128), BF16),
            pltpu.VMEM((4, 32, 128), BF16),
            pltpu.VMEM((4, 32, 128), BF16),
            pltpu.VMEM((2, 4, 4, 4, 32, 128), BF16),
            pltpu.VMEM((4, 32, 128), BF16),
            pltpu.VMEM((4, 4, 8, 32, 128), BF16),
            pltpu.VMEM((4, 8, 32, 128), BF16),
            pltpu.VMEM((4, 8, 32, 128), BF16),
            pltpu.VMEM((8, 8, 128), F32),
            pltpu.VMEM((2, 4, 4, 2, 64, 128), BF16),
            pltpu.VMEM((2, 2, 2, 64, 128), BF16),
            pltpu.VMEM((2, 2, 2, 64, 128), BF16),
            pltpu.VMEM((2, 4, 2, 64, 128), BF16),
            pltpu.VMEM((2, 4, 2, 64, 128), BF16),
            pltpu.VMEM((2, 4, 2, 64, 128), F32),
            pltpu.VMEM((2, 4, 2, 64, 128), BF16),
            pltpu.VMEM((2, 3, 2, 64, 128), BF16),
            pltpu.VMEM((2, 2, 64, 128), F32),
            pltpu.VMEM((2, 64, 128), BF16),
            pltpu.VMEM((2, 64, 128), BF16),
            pltpu.VMEM((128, 256), F32),
            pltpu.VMEM((128, 128), F32),
            pltpu.VMEM((4, 128, 128), F32),
            pltpu.SemaphoreType.DMA((N_SEMS,)),
            pltpu.SemaphoreType.DMA((N_SEMS,)),
            pltpu.SemaphoreType.DMA((2,)),
        ],
        compiler_params=pltpu.CompilerParams(collective_id=0, has_side_effects=True),
        name="cross_layer",
    )(
        base_rows,
        layer_rows.reshape(4, 32, 128),
        upstream,
        cross_bias.reshape(1, 128),
        cross_weight.reshape(32, 2, 128, 128),
    )
    return crossed, gbase, glayer, gw.reshape(1024, 128), gbias.reshape(128)


def solution(mesh):
    return jax.shard_map(
        local,
        mesh=mesh,
        in_specs=(P("dp", "mp"), P("dp", "mp"), P(None, "mp"), P("mp"), P("dp", "mp")),
        out_specs=(P("dp", "mp"), P("dp", "mp"), P("dp", "mp"), P("dp", "mp"), P("mp")),
        check_vma=False,
    )
```

time: 345 us -> 61.3 us (0.18)
  waiting for transfers between devices: 189 us -> 0 us
  blocking collectives: 99.6 us -> 0 us
  Pallas kernels: 0 us -> 53.1 us
  between operations: 15.6 us -> 0.64 us
  local copies, waits for them, and re-layouts: 18.2 us -> 7.09 us
  matrix products: 10.8 us -> 0 us
  starting transfers between devices: 9.81 us -> 0 us
    all_to_all x2 -> x0, waiting for transfers between devices: 189 us -> none  [the longest x1 174 us: sent_to_all(): lax.all_to_all(jnp.broadcast_to(value[None], (size, *value.shape)), axis,...]
    all_to_all x3 -> x0, blocking collectives: 99.6 us -> none  [sent_to_all(): lax.all_to_all(jnp.broadcast_to(value[None], (size, *value.shape)), axis,...]
    pallas_call x0 -> x1, Pallas kernels: none -> 53.1 us  [local(): pl.pallas_call(functools.partial(kernel, scale), out_shape=(small, small,...]
    dot_general x3 -> x0, matrix products: 10.8 us -> none  [the longest x1 4.26 us: local(): lax.dot_general(full_rows, delta_low, (((0,), (0,)), ((), ())), preferred...]
    all_to_all x2 -> x0, starting transfers between devices: 9.73 us -> none  [the longest x1 5.39 us: local(): lax.all_to_all(own_cols, MP, split_axis=0, concat_axis=1, tiled=True)]
    transpose x2 -> x0, local copies, waits for them, and re-layouts: 7.74 us -> none  [the longest x1 4.17 us: joined_along(): return jnp.moveaxis(parts, 0, dim).reshape(shape)]
    unnamed x13 -> x5, local copies, waits for them, and re-layouts: 1.02 us -> 7.09 us
    all_to_all x2 -> x0, local copies, waits for them, and re-layouts: 3.99 us -> none  [the longest x1 2.51 us: local(): lax.all_to_all(own_cols, MP, split_axis=0, concat_axis=1, tiled=True)]
  transfers between devices with their start and end apart: 4 -> 0, of which waited for: 2 -> 0; matrix products, arithmetic and copies ran while one was open for 5% -> 0% of each run, Pallas kernels for 0% -> 0%
where the time goes in v1:
time: 61.3 us; the launch traced here: 60.9 us
  Pallas kernels  53.1 us (87%)
  local copies, waits for them, and re-layouts  7.09 us (12%)
  between operations  0.64 us (1%)
    pallas_call x1, Pallas kernels, local(): pl.pallas_call(functools.partial(kernel, scale), out_shape=(small, small,...  53.1 us
    unnamed x5, local copies, waits for them, and re-layouts  7.09 us

profile of v1, /device:TPU:1, one launch (start us, length us, event | category | flops | bytes accessed | tf_op | source)
XLA Modules:
  0.0 60.9 jit_solution(13869439108881603386)
XLA Ops:
  0.6 53.1 %cross_layer.1 = (bf16[128,128]{1,0:T(8,128)(2,1)}, bf16[128,128]{1,0:T(8,128)(2,1)}, bf16[128,128]{1,0:T(8,128)(2,1)}, f32[4,2,128,128]{3,2,1,0:T(8,128)}, f32[1,128]{1,0:T(1,128)}) custom-call(bf16[128,128]{1,0:T(8,128)(2,1)} %base.1, bf16[4,32,128]{2,1,0:T(8,128)(2,1)} %bitcast.7, bf16[128,128]{1,0:T(8,128)(2,1)} %up.1, f32[1,128]{1,0:T(1,128)} %bitcast.8, ...), custom_call_target="tpu_custom_call" | custom-call | tf_op jit(solution)/shard_map/cross_layer/pallas_call | solution.py:405
  53.8 1.4 %copy.15 = bf16[128,128]{1,0:T(8,128)(2,1)} copy(bf16[128,128]{1,0:T(8,128)(2,1)} %get-tuple-element.20) | data formatting | bytes 65536
  55.1 1.4 %copy.16 = bf16[128,128]{1,0:T(8,128)(2,1)} copy(bf16[128,128]{1,0:T(8,128)(2,1)} %get-tuple-element.21) | data formatting | bytes 65536
  56.5 1.4 %copy.17 = bf16[128,128]{1,0:T(8,128)(2,1)} copy(bf16[128,128]{1,0:T(8,128)(2,1)} %get-tuple-element.22) | data formatting | bytes 65536
  57.9 1.9 %copy.18 = f32[1024,128]{1,0:T(8,128)} copy(f32[1024,128]{1,0:T(8,128)} %bitcast.6) | data formatting | bytes 1048576
  59.7 1.1 %copy.19 = f32[128]{0:T(128)} copy(f32[128]{0:T(128)} %bitcast.9) | data formatting | bytes 1024

commit v2 on v1

--- a/solution.py
+++ b/solution.py
@@ -15,16 +15,20 @@
 
 def kernel(
     scale,
-    base,
-    lay,
-    up,
-    bias,
+    base_hbm,
+    lay_hbm,
+    up_hbm,
+    bias_hbm,
     w4,
     crossed,
     gbase,
     glayer,
     gw,
     gbias,
+    base,
+    lay,
+    up,
+    bias,
     wo,
     wp,
     dl,
@@ -100,11 +104,6 @@
             device_id_type=MESH,
         ).wait_recv()
 
-    load_w = pltpu.make_async_copy(w4.at[:, c], wo, lsem.at[0])
-    load_w.start()
-    own_x = pltpu.make_async_copy(lay, xa.at[h, x, y], lsem.at[1])
-    own_x.start()
-
     barrier = pltpu.get_barrier_semaphore()
     near = [dev(c_=oc)]
     near += [dev(x_=plus(x, k)) for k in (1, 2, 3)]
@@ -116,6 +115,24 @@
     for to in near:
         pl.semaphore_signal(barrier, inc=1, device_id=to, device_id_type=MESH)
 
+    loads = [
+        pltpu.make_async_copy(src, dst, lsem.at[k])
+        for k, (src, dst) in enumerate(
+            (
+                (up_hbm, up),
+                (base_hbm, base),
+                (lay_hbm, lay),
+                (lay_hbm, xa.at[h, x, y]),
+                (bias_hbm, bias),
+                (w4.at[:, c], wo),
+            )
+        )
+    ]
+    for load in loads:
+        load.start()
+    loads[0].wait()
+    loads[1].wait()
+
     upper = up[...].astype(F32)
     basef = base[...].astype(F32)
     delta = upper * basef
@@ -124,7 +141,8 @@
     do[:, d] = low
     bs[d] = jnp.broadcast_to(jnp.sum(delta, axis=0, keepdims=True), (8, 128))
 
-    own_x.wait()
+    loads[2].wait()
+    loads[3].wait()
     pl.semaphore_wait(barrier, len(near))
 
     k_dlp = put(dl, dlp, dev(c_=oc))
@@ -239,7 +257,7 @@
     ag1_wait(x_own, 4, own1)
     own2 = ag2(x_own, 4)
 
-    load_w.wait()
+    loads[5].wait()
     got(k_dlp, dlp)
     d_own = dl[...].reshape(128, 128)
     d_other = dlp[...].reshape(128, 128)
@@ -380,6 +398,7 @@
     gbias[...] = jnp.sum(bs[:, 0], axis=0, keepdims=True) * scale
 
     got(k_mix, mixr)
+    loads[4].wait()
     mixed = mixp[:, 0:128] + mixr[...] + bias[...]
     crossed[...] = (basef * mixed + lay[...].reshape(128, 128).astype(F32)).astype(BF16)
     gbase[...] = (upper * mixed).astype(BF16)
@@ -398,22 +417,39 @@
             copy.wait_send()
 
 
+def finish(a, b, e, g, s, oa, ob, oe, og, os_, sem):
+    copies = [
+        pltpu.make_async_copy(src, dst, sem.at[k])
+        for k, (src, dst) in enumerate(((g, og), (a, oa), (b, ob), (e, oe), (s, os_)))
+    ]
+    for copy in copies:
+        copy.start()
+    for copy in copies:
+        copy.wait()
+
+
 def local(base_rows, layer_rows, cross_weight, cross_bias, upstream):
     vmem = pl.BlockSpec(memory_space=pltpu.VMEM)
+    hbm = pl.BlockSpec(memory_space=pltpu.HBM)
     scale = float((base_rows.shape[0] * 8) ** -0.5)
     small = jax.ShapeDtypeStruct((128, 128), BF16)
-    crossed, gbase, glayer, gw, gbias = pl.pallas_call(
+    shapes = (
+        small,
+        small,
+        small,
+        jax.ShapeDtypeStruct((4, 2, 128, 128), F32),
+        jax.ShapeDtypeStruct((1, 128), F32),
+    )
+    results = pl.pallas_call(
         functools.partial(kernel, scale),
-        out_shape=(
-            small,
-            small,
-            small,
-            jax.ShapeDtypeStruct((4, 2, 128, 128), F32),
-            jax.ShapeDtypeStruct((1, 128), F32),
-        ),
-        in_specs=[vmem, vmem, vmem, vmem, pl.BlockSpec(memory_space=pl.ANY)],
+        out_shape=shapes,
+        in_specs=[hbm] * 5,
         out_specs=(vmem, vmem, vmem, vmem, vmem),
         scratch_shapes=[
+            pltpu.VMEM((128, 128), BF16),
+            pltpu.VMEM((4, 32, 128), BF16),
+            pltpu.VMEM((128, 128), BF16),
+            pltpu.VMEM((1, 128), F32),
             pltpu.VMEM((32, 128, 128), BF16),
             pltpu.VMEM((32, 128, 128), BF16),
             pltpu.VMEM((4, 32, 128), BF16),
@@ -440,17 +476,33 @@
             pltpu.VMEM((4, 128, 128), F32),
             pltpu.SemaphoreType.DMA((N_SEMS,)),
             pltpu.SemaphoreType.DMA((N_SEMS,)),
-            pltpu.SemaphoreType.DMA((2,)),
+            pltpu.SemaphoreType.DMA((6,)),
         ],
-        compiler_params=pltpu.CompilerParams(collective_id=0, has_side_effects=True),
+        compiler_params=pltpu.CompilerParams(
+            collective_id=0, has_side_effects=True, vmem_limit_bytes=24 << 20
+        ),
         name="cross_layer",
     )(
-        base_rows,
-        layer_rows.reshape(4, 32, 128),
-        upstream,
-        cross_bias.reshape(1, 128),
-        cross_weight.reshape(32, 2, 128, 128),
+        *(
+            pltpu.with_memory_space_constraint(a, pltpu.HBM)
+            for a in (
+                base_rows,
+                layer_rows.reshape(4, 32, 128),
+                upstream,
+                cross_bias.reshape(1, 128),
+                cross_weight.reshape(32, 2, 128, 128),
+            )
+        )
     )
+    crossed, gbase, glayer, gw, gbias = pl.pallas_call(
+        finish,
+        out_shape=shapes,
+        in_specs=[vmem] * 5,
+        out_specs=(pl.BlockSpec(memory_space=pl.ANY),) * 5,
+        scratch_shapes=[pltpu.SemaphoreType.DMA((5,))],
+        compiler_params=pltpu.CompilerParams(vmem_limit_bytes=4 << 20),
+        name="finish",
+    )(*results)
     return crossed, gbase, glayer, gw.reshape(1024, 128), gbias.reshape(128)
 
 

time: 61.3 us -> 53.2 us (0.87)
  local copies, waits for them, and re-layouts: 7.09 us -> 0 us
  Pallas kernels: 53.1 us -> 52.4 us
    unnamed x5 -> x0, local copies, waits for them, and re-layouts: 7.09 us -> none
    pallas_call x1 -> x2, Pallas kernels: 53.1 us -> 52.4 us  [the longest x1 51.5 us: local(): pl.pallas_call(functools.partial(kernel, scale), out_shape=shapes, in_spe...]
where the time goes in v2:
time: 53.2 us; the launch traced here: 53 us
  Pallas kernels  52.4 us (98%)
  between operations  0.64 us (1%)
    pallas_call x1, Pallas kernels, local(): pl.pallas_call(functools.partial(kernel, scale), out_shape=shapes, in_spe...  51.5 us

profile of v2, /device:TPU:1, one launch (start us, length us, event | category | flops | bytes accessed | tf_op | source)
XLA Modules:
  0.0 53.0 jit_solution(15869034603340498160)
XLA Ops:
  0.6 51.5 %cross_layer.1 = (bf16[128,128]{1,0:T(8,128)(2,1)S(1)}, bf16[128,128]{1,0:T(8,128)(2,1)S(1)}, bf16[128,128]{1,0:T(8,128)(2,1)S(1)}, f32[4,2,128,128]{3,2,1,0:T(8,128)S(1)}, f32[1,128]{1,0:T(1,128)S(1)}) custom-call(bf16[128,128]{1,0:T(8,128)(2,1)} %base_hbm.1, bf16[4,32,128]{2,1,0:T(8,128)(2,1)} %bitcast.6, bf16[128,128]{1,0:T(8,128)(2,1)} %up_hbm.1, ...), custom_call_target="tpu_custom_call" | custom-call | tf_op jit(solution)/shard_map/cross_layer/pallas_call | solution.py:443
  52.2 0.9 %finish.1 = (bf16[128,128]{1,0:T(8,128)(2,1)}, bf16[128,128]{1,0:T(8,128)(2,1)}, bf16[128,128]{1,0:T(8,128)(2,1)}, f32[4,2,128,128]{3,2,1,0:T(8,128)}, f32[1,128]{1,0:T(1,128)}) custom-call(bf16[128,128]{1,0:T(8,128)(2,1)S(1)} %get-tuple-element.15.a, bf16[128,128]{1,0:T(8,128)(2,1)S(1)} %get-tuple-element.16.b, bf16[128,128]{1,0:T(8,128)(2,1)S(1)} %get-tuple-element.17.e, ...), custom_call_target="tpu_custom_call" | custom-call | tf_op jit(solution)/shard_map/finish/pallas_call | solution.py:497

commit v3 on v2

v3 whole, which is shorter than its diff:
```python
import functools
import math

import jax
import jax.numpy as jnp
from jax import lax
from jax.experimental import pallas as pl
from jax.experimental.pallas import tpu as pltpu
from jax.sharding import PartitionSpec as P

MESH = pl.DeviceIdType.MESH
F32 = jnp.float32
BF16 = jnp.bfloat16
N_SENDS = 14
N_RECVS = 49
MOST_ROWS = 4096


def kernel(
    scale,
    base_hbm,
    lay_hbm,
    up_hbm,
    bias_hbm,
    w4,
    crossed,
    gbase,
    glayer,
    gw,
    gbias,
    base,
    lay,
    up,
    bias,
    wo,
    wp,
    dl,
    dlp,
    xa,
    xb,
    do,
    dp_,
    bs,
    part,
    r1lo,
    r1hi,
    rl,
    rr,
    s1,
    b2s,
    r2,
    tt,
    zs,
    zr,
    mixp,
    mixr,
    gws,
    tally,
    send,
    recv,
    lsem,
):
    d = lax.axis_index("dp")
    m = lax.axis_index("mp")
    c = lax.rem(m, 2)
    y = lax.rem(lax.div(m, 2), 4)
    h = lax.rem(lax.div(m, 8), 2)
    x = lax.div(m, 16)
    oh = 1 - h
    oc = 1 - c

    def dev(x_=None, y_=None, h_=None, c_=None, d_=None):
        x_ = x if x_ is None else x_
        y_ = y if y_ is None else y_
        h_ = h if h_ is None else h_
        c_ = c if c_ is None else c_
        d_ = d if d_ is None else d_
        return (d_, ((x_ * 2 + h_) * 4 + y_) * 2 + c_)

    def plus(v, k):
        return lax.rem(v + k, 4)

    ids = iter(range(N_RECVS))
    send_ids = iter(range(N_SENDS))
    sent = [[next(send_ids), 0]]

    def rows(ref):
        return math.prod(ref.shape) * jnp.dtype(ref.dtype).itemsize // 256

    def wait_rows(sem, n):
        view = tally.at[pl.ds(0, n)]
        pltpu.make_async_copy(view, view, sem).wait()

    def put(src, dst, to, k=None):
        k = next(ids) if k is None else k
        n = rows(src)
        if sent[-1][1] + n > MOST_ROWS:
            sent.append([next(send_ids), 0])
        sent[-1][1] += n
        pltpu.make_async_remote_copy(
            src_ref=src,
            dst_ref=dst,
            send_sem=send.at[sent[-1][0]],
            recv_sem=recv.at[k],
            device_id=to,
            device_id_type=MESH,
        ).start()
        return k

    def got(k, *landed):
        wait_rows(recv.at[k], sum(rows(ref) for ref in landed))

    b4, b2, b1 = lax.div(d, 4), lax.rem(lax.div(d, 2), 2), lax.rem(d, 2)
    mine = d == 2 * x + h

    def first_row(d_, h_):
        window = jnp.clip(d_ - 2, 0, 4)
        return jnp.where(lax.rem(d_, 2) == h_, window, window + 4)

    barrier = pltpu.get_barrier_semaphore()
    near = [dev(c_=oc)]
    near += [dev(x_=plus(x, k)) for k in (1, 2, 3)]
    near += [dev(y_=plus(y, k)) for k in (1, 2, 3)]
    near += [dev(h_=oh), dev(d_=d + 4 - 8 * b4), dev(d_=d + 2 - 4 * b2), dev(d_=d + 1 - 2 * b1)]
    for to in near:
        pl.semaphore_signal(barrier, inc=1, device_id=to, device_id_type=MESH)
    z_to = []
    for t in range(4):
        for hh in (0, 1):
            same = jnp.logical_and(x == t, jnp.logical_and(h == hh, mine))
            z_to.append((t, hh, same, dev(x_=t, h_=hh, d_=2 * x + h)))
    z_from = []
    for s in range(8):
        same = jnp.logical_and(d == s, mine)
        z_from.append((same, dev(x_=lax.div(d, 2), h_=lax.rem(d, 2), d_=s)))
    for same, to in [(same, to) for _, _, same, to in z_to] + z_from:

        @pl.when(jnp.logical_not(same))
        def _(to=to):
            pl.semaphore_signal(barrier, inc=1, device_id=to, device_id_type=MESH)

    n_signals = len(near) + 16 - 2 * mine.astype(jnp.int32)

    loads = [
        pltpu.make_async_copy(src, dst, lsem.at[k])
        for k, (src, dst) in enumerate(
            (
                (lay_hbm, lay),
                (up_hbm, up),
                (base_hbm, base),
                (lay_hbm, xa.at[h, x, y]),
                (bias_hbm, bias),
                (w4.at[:, :, :, c], wo),
            )
        )
    ]
    for load in loads:
        load.start()
    loads[0].wait()
    pl.semaphore_wait(barrier, n_signals)

    def ag1(view, n):
        half = n // 2
        k = next(ids)
        for j in (1, 3, 2):
            a = view(x, y, 0, half)
            b = view(x, y, half, half)
            put(a, a, dev(x_=plus(x, j)), k)
            put(b, b, dev(y_=plus(y, j)), k)
        return k

    def ag1_wait(view, n, k):
        half = n // 2
        got(k, *[view(x, y, 0, half)] * 3, *[view(x, y, half, half)] * 3)

    every = pl.ds(0, 4)

    def ag2(view, n):
        half = n // 2
        ks = []
        for j in (1, 3):
            a = view(every, y, 0, half)
            b = view(x, every, half, half)
            ks.append((put(a, a, dev(y_=plus(y, j))), put(b, b, dev(x_=plus(x, j)))))
        return ks

    def ag2_forward(view, n, ks):
        half = n // 2
        k = next(ids)
        for (ka, kb), j, part_of in zip(ks, (1, 3), (pl.ds(0, 2), pl.ds(2, 2)), strict=True):
            ys, xs = plus(y, 4 - j), plus(x, 4 - j)
            got(ka, view(every, ys, 0, half))
            a = view(part_of, ys, 0, half)
            put(a, a, dev(y_=plus(y, j)), k)
            got(kb, view(xs, every, half, half))
            b = view(xs, part_of, half, half)
            put(b, b, dev(x_=plus(x, j)), k)
        return k

    def ag2_wait(view, n, k):
        half = n // 2
        got(k, view(every, y, 0, half), view(x, every, half, half))

    def x_own(xs, ys, q, nq):
        return xa.at[h, xs, ys, pl.ds(q, nq)]

    def x_other(xs, ys, q, nq):
        return xa.at[oh, xs, ys, pl.ds(q, nq)]

    def x_block0(xs, ys, q, nq):
        return xb.at[xs, ys, pl.ds(q, nq)]

    def x_block1(xs, ys, q, nq):
        return xb.at[xs, ys, pl.ds(4 + q, nq)]

    z_first = [next(send_ids) for _ in range(8)]
    z_recv = next(ids)
    next(ids)
    z_sent = []
    for n, (t, hh, same, to) in enumerate(z_to):
        d_to = 2 * x + h
        slot = lax.rem(d + 8 - first_row(d_to, hh), 8)
        src, dst = lay.at[t], xb.at[t, y, slot]
        copy = pltpu.make_async_remote_copy(
            src_ref=src,
            dst_ref=dst,
            send_sem=send.at[z_first[n]],
            recv_sem=recv.at[z_recv + lax.div(slot, 4)],
            device_id=to,
            device_id_type=MESH,
        )
        stay = pltpu.make_async_copy(src, dst, recv.at[z_recv + lax.div(slot, 4)])

        @pl.when(same)
        def _(stay=stay):
            stay.start()

        @pl.when(jnp.logical_not(same))
        def _(copy=copy):
            copy.start()

        z_sent.append((same, copy))

    k_zx = put(lay, xa.at[h, x, y], dev(h_=oh))
    k_wp = [put(w4.at[:, oh, :, oc], wp.at[:, oh], dev(c_=oc))]
    loads[3].wait()
    own1 = ag1(x_own, 4)

    loads[1].wait()
    loads[2].wait()
    upper = up[...].astype(F32)
    basef = base[...].astype(F32)
    delta = upper * basef
    low = delta.astype(BF16).reshape(4, 32, 128)
    dl[...] = low
    do[:, b4, b2, b1] = low
    bs[b4, b2, b1] = jnp.broadcast_to(jnp.sum(delta, axis=0, keepdims=True), (8, 128))
    k_dlp = put(dl, dlp, dev(c_=oc))
    k_wp.append(put(w4.at[:, h, :, oc], wp.at[:, h], dev(c_=oc)))

    every2 = pl.ds(0, 2)
    steps = (
        (dev(d_=d + 4 - 8 * b4), (b4, b2, b1), (1 - b4, b2, b1)),
        (dev(d_=d + 2 - 4 * b2), (every2, b2, b1), (every2, 1 - b2, b1)),
        (dev(d_=d + 1 - 2 * b1), (every2, every2, b1), (every2, every2, 1 - b1)),
    )

    def along_z(step):
        to, here, _ = steps[step]
        a, b = do.at[(slice(None), *here)], bs.at[here]
        return put(b, b, to, put(a, a, to))

    def along_z_wait(step, k):
        theirs = steps[step][2]
        got(k, do.at[(slice(None), *theirs)], bs.at[theirs])

    k_d = along_z(0)

    loads[5].wait()
    got(k_dlp, dlp)
    d_own = dl[...].reshape(128, 128)
    d_other = dlp[...].reshape(128, 128)
    nt = (((1,), (1,)), ((), ()))
    lo, hi = pl.ds(0, 2), pl.ds(2, 2)

    def to_line(half, j):
        return dev(x_=plus(x, j)) if half == 0 else dev(y_=plus(y, j))

    def to_line2(half, j):
        return dev(y_=plus(y, j)) if half == 0 else dev(x_=plus(x, j))

    def back_terms(hs):
        for xs in range(4):
            term = lax.dot_general(
                wo[xs, hs].reshape(512, 128), d_own, nt, preferred_element_type=F32
            ) + lax.dot_general(
                wp[xs, hs].reshape(512, 128), d_other, nt, preferred_element_type=F32
            )
            term = term.astype(BF16).reshape(4, 128, 128)
            part[hs, 0, xs] = term[:, 0:64]
            for ys in range(4):
                part[hs, 1, ys, xs] = term[ys, 64:128]

    def rs1(hs):
        first, rest = [], next(ids)
        for half in (0, 1):
            me = x if half == 0 else y
            a = put(part.at[hs, half, plus(me, 2), lo], r1lo.at[hs, half], to_line(half, 1))
            b = put(part.at[hs, half, plus(me, 2), hi], r1hi.at[hs, half], to_line(half, 3))
            first.append((a, b))
        for half in (0, 1):
            me = x if half == 0 else y
            put(part.at[hs, half, plus(me, 1), hi], rl.at[hs, half, hi], to_line(half, 1), rest)
            put(part.at[hs, half, plus(me, 3), lo], rr.at[hs, half, lo], to_line(half, 3), rest)
        return first, rest

    def rs2(hs, ks):
        first, rest = ks
        for half in (0, 1):
            me = x if half == 0 else y
            a, b = first[half]
            got(a, r1lo.at[hs, half])
            t = plus(me, 1)
            part[hs, half, t, lo] = (
                part[hs, half, t, lo].astype(F32) + r1lo[hs, half].astype(F32)
            ).astype(BF16)
            put(part.at[hs, half, t, lo], rl.at[hs, half, lo], to_line(half, 1), rest)
            got(b, r1hi.at[hs, half])
            t = plus(me, 3)
            part[hs, half, t, hi] = (
                part[hs, half, t, hi].astype(F32) + r1hi[hs, half].astype(F32)
            ).astype(BF16)
            put(part.at[hs, half, t, hi], rr.at[hs, half, hi], to_line(half, 3), rest)
        return rest

    def rs3(hs, rest):
        got(rest, rl.at[hs], rr.at[hs])
        k = next(ids)
        for half in (0, 1):
            me, me2 = (x, y) if half == 0 else (y, x)
            total = (
                part[hs, half, me].astype(F32)
                + rl[hs, half].astype(F32)
                + rr[hs, half].astype(F32)
            )
            s1[hs, half] = total
            b2s[hs, half] = total.astype(BF16)
            for j in (1, 3, 2):
                t = plus(me2, j)
                put(b2s.at[hs, half, t], r2.at[hs, half, j - 1], to_line2(half, j), k)
        return k

    def rs4(hs, k):
        got(k, r2.at[hs])
        for half in (0, 1):
            me2 = y if half == 0 else x
            tt[hs, half] = (
                s1[hs, half, me2]
                + r2[hs, half, 0].astype(F32)
                + r2[hs, half, 1].astype(F32)
                + r2[hs, half, 2].astype(F32)
            )

    got(k_wp[0], wp.at[:, oh])
    back_terms(oh)
    k_far = rs1(oh)
    got(k_wp[1], wp.at[:, h])
    back_terms(h)
    k_near = rs1(h)

    ag1_wait(x_own, 4, own1)
    own2 = ag2(x_own, 4)
    k_far = rs2(oh, k_far)
    k_near = rs2(h, k_near)

    def mixed_terms(hs, acc):
        for xs in range(4):
            rows = jnp.concatenate([xa[hs, xs, ys].reshape(128, 128) for ys in range(4)], axis=1)
            cols = jnp.concatenate(
                [wo[xs, hs].reshape(512, 128), wp[xs, hs].reshape(512, 128)], axis=1
            )
            acc = acc + jnp.dot(rows, cols, preferred_element_type=F32)
        return acc

    quarter = xb.at[x, y, pl.ds(0, 4)]
    got(z_recv, quarter)
    first1 = ag1(x_block0, 4)
    got(k_zx, xa.at[oh, x, y])
    other1 = ag1(x_other, 4)
    k_far = rs3(oh, k_far)
    got(z_recv + 1, quarter)
    second1 = ag1(x_block1, 4)
    k_near = rs3(h, k_near)

    along_z_wait(0, k_d)
    k_d = along_z(1)
    own3 = ag2_forward(x_own, 4, own2)
    ag1_wait(x_block0, 4, first1)
    first2 = ag2(x_block0, 4)
    ag1_wait(x_other, 4, other1)
    other2 = ag2(x_other, 4)

    rs4(oh, k_far)
    zs[...] = tt[oh].astype(BF16)
    k_zr = put(zs, zr, dev(h_=oh))

    ag1_wait(x_block1, 4, second1)
    second2 = ag2(x_block1, 4)
    along_z_wait(1, k_d)
    k_d = along_z(2)
    ag2_wait(x_own, 4, own3)
    mixp[...] = mixed_terms(h, jnp.zeros((128, 256), F32))

    first3 = ag2_forward(x_block0, 4, first2)
    other3 = ag2_forward(x_other, 4, other2)
    rs4(h, k_near)
    second3 = ag2_forward(x_block1, 4, second2)
    along_z_wait(2, k_d)
    k_dp = put(do, dp_, dev(c_=oc))

    ag2_wait(x_other, 4, other3)
    mixp[...] = mixed_terms(oh, mixp[...])
    k_mix = put(mixp.at[:, pl.ds(128, 128)], mixr, dev(c_=oc))

    tn = (((0,), (0,)), ((), ()))

    def rows_of(ref, xs, g):
        out = []
        for k in range(4):
            s = lax.rem(first_row(d, h) + 4 * g + k, 8)
            out.append(ref[xs, lax.div(s, 4), lax.rem(lax.div(s, 2), 2), lax.rem(s, 2)])
        return jnp.concatenate(out, axis=0)

    def weight_terms(g):
        feats = jnp.concatenate(
            [
                jnp.concatenate(
                    [xb[xs, ys, 4 * g : 4 * g + 4].reshape(128, 128) for ys in range(4)], axis=1
                )
                for xs in range(4)
            ],
            axis=0,
        )
        cols = jnp.concatenate(
            [
                jnp.concatenate(
                    [rows_of(do, xs, g), rows_of(dp_, xs, g)], axis=1
                )
                for xs in range(4)
            ],
            axis=0,
        )
        return lax.dot_general(feats, cols, tn, preferred_element_type=F32)

    got(k_dp, dp_)
    ag2_wait(x_block0, 4, first3)
    acc = weight_terms(0)
    ag2_wait(x_block1, 4, second3)
    acc = acc + weight_terms(1)
    acc = acc * scale
    gws[...] = acc[:, 128:256].reshape(4, 128, 128)
    k_gw = put(gws, gw.at[:, c], dev(c_=oc))
    gw[:, c] = acc[:, 0:128].reshape(4, 128, 128)

    gbias[...] = jnp.sum(bs[...].reshape(8, 8, 128)[:, 0], axis=0, keepdims=True) * scale

    got(k_mix, mixr)
    loads[4].wait()
    mixed = mixp[:, 0:128] + mixr[...] + bias[...]
    crossed[...] = (basef * mixed + lay[...].reshape(128, 128).astype(F32)).astype(BF16)
    gbase[...] = (upper * mixed).astype(BF16)

    got(k_zr, zr)
    back = (tt[h] + zr[...].astype(F32)).reshape(128, 128)
    glayer[...] = (upper + back.T).astype(BF16)

    got(k_gw, gw.at[:, oc])
    for k, n in sent:
        wait_rows(send.at[k], n)
    for same, copy in z_sent:

        @pl.when(jnp.logical_not(same))
        def _(copy=copy):
            copy.wait_send()


def finish(a, b, e, g, s, oa, ob, oe, og, os_, sem):
    copies = [
        pltpu.make_async_copy(src, dst, sem.at[k])
        for k, (src, dst) in enumerate(((g, og), (a, oa), (b, ob), (e, oe), (s, os_)))
    ]
    for copy in copies:
        copy.start()
    for copy in copies:
        copy.wait()


def local(base_rows, layer_rows, cross_weight, cross_bias, upstream):
    vmem = pl.BlockSpec(memory_space=pltpu.VMEM)
    hbm = pl.BlockSpec(memory_space=pltpu.HBM)
    scale = float((base_rows.shape[0] * 8) ** -0.5)
    small = jax.ShapeDtypeStruct((128, 128), BF16)
    shapes = (
        small,
        small,
        small,
        jax.ShapeDtypeStruct((4, 2, 128, 128), F32),
        jax.ShapeDtypeStruct((1, 128), F32),
    )
    results = pl.pallas_call(
        functools.partial(kernel, scale),
        out_shape=shapes,
        in_specs=[hbm] * 5,
        out_specs=(vmem, vmem, vmem, vmem, vmem),
        scratch_shapes=[
            pltpu.VMEM((128, 128), BF16),
            pltpu.VMEM((4, 32, 128), BF16),
            pltpu.VMEM((128, 128), BF16),
            pltpu.VMEM((1, 128), F32),
            pltpu.VMEM((4, 2, 4, 128, 128), BF16),
            pltpu.VMEM((4, 2, 4, 128, 128), BF16),
            pltpu.VMEM((4, 32, 128), BF16),
            pltpu.VMEM((4, 32, 128), BF16),
            pltpu.VMEM((2, 4, 4, 4, 32, 128), BF16),
            pltpu.VMEM((4, 4, 8, 32, 128), BF16),
            pltpu.VMEM((4, 2, 2, 2, 32, 128), BF16),
            pltpu.VMEM((4, 2, 2, 2, 32, 128), BF16),
            pltpu.VMEM((2, 2, 2, 8, 128), F32),
            pltpu.VMEM((2, 2, 4, 4, 64, 128), BF16),
            pltpu.VMEM((2, 2, 2, 64, 128), BF16),
            pltpu.VMEM((2, 2, 2, 64, 128), BF16),
            pltpu.VMEM((2, 2, 4, 64, 128), BF16),
            pltpu.VMEM((2, 2, 4, 64, 128), BF16),
            pltpu.VMEM((2, 2, 4, 64, 128), F32),
            pltpu.VMEM((2, 2, 4, 64, 128), BF16),
            pltpu.VMEM((2, 2, 3, 64, 128), BF16),
            pltpu.VMEM((2, 2, 64, 128), F32),
            pltpu.VMEM((2, 64, 128), BF16),
            pltpu.VMEM((2, 64, 128), BF16),
            pltpu.VMEM((128, 256), F32),
            pltpu.VMEM((128, 128), F32),
            pltpu.VMEM((4, 128, 128), F32),
            pltpu.VMEM((2 * MOST_ROWS, 128), BF16),
            pltpu.SemaphoreType.DMA((N_SENDS,)),
            pltpu.SemaphoreType.DMA((N_RECVS,)),
            pltpu.SemaphoreType.DMA((6,)),
        ],
        compiler_params=pltpu.CompilerParams(
            collective_id=0, has_side_effects=True, vmem_limit_bytes=24 << 20
        ),
        name="cross_layer",
    )(
        *(
            pltpu.with_memory_space_constraint(a, pltpu.HBM)
            for a in (
                base_rows,
                layer_rows.reshape(4, 32, 128),
                upstream,
                cross_bias.reshape(1, 128),
                cross_weight.reshape(4, 2, 4, 2, 128, 128),
            )
        )
    )
    crossed, gbase, glayer, gw, gbias = pl.pallas_call(
        finish,
        out_shape=shapes,
        in_specs=[vmem] * 5,
        out_specs=(pl.BlockSpec(memory_space=pl.ANY),) * 5,
        scratch_shapes=[pltpu.SemaphoreType.DMA((5,))],
        compiler_params=pltpu.CompilerParams(vmem_limit_bytes=4 << 20),
        name="finish",
    )(*results)
    return crossed, gbase, glayer, gw.reshape(1024, 128), gbias.reshape(128)


def solution(mesh):
    return jax.shard_map(
        local,
        mesh=mesh,
        in_specs=(P("dp", "mp"), P("dp", "mp"), P(None, "mp"), P("mp"), P("dp", "mp")),
        out_specs=(P("dp", "mp"), P("dp", "mp"), P("dp", "mp"), P("dp", "mp"), P("mp")),
        check_vma=False,
    )
```

time: 53.2 us -> 48.5 us (0.912)
  Pallas kernels: 52.4 us -> 47.8 us
    pallas_call x1, Pallas kernels: 51.5 us -> 46.9 us  [local(): pl.pallas_call(functools.partial(kernel, scale), out_shape=shapes, in_spe...]
where the time goes in v3:
time: 48.5 us; the launch traced here: 48.4 us
  Pallas kernels  47.8 us (99%)
  between operations  0.64 us (1%)
    pallas_call x1, Pallas kernels, local(): pl.pallas_call(functools.partial(kernel, scale), out_shape=shapes, in_spe...  46.9 us

profile of v3, /device:TPU:1, one launch (start us, length us, event | category | flops | bytes accessed | tf_op | source)
XLA Modules:
  0.0 48.4 jit_solution(956350110897023951)
XLA Ops:
  0.6 46.9 %cross_layer.1 = (bf16[128,128]{1,0:T(8,128)(2,1)S(1)}, bf16[128,128]{1,0:T(8,128)(2,1)S(1)}, bf16[128,128]{1,0:T(8,128)(2,1)S(1)}, f32[4,2,128,128]{3,2,1,0:T(8,128)S(1)}, f32[1,128]{1,0:T(1,128)S(1)}) custom-call(bf16[128,128]{1,0:T(8,128)(2,1)} %base_hbm.1, bf16[4,32,128]{2,1,0:T(8,128)(2,1)} %bitcast.6, bf16[128,128]{1,0:T(8,128)(2,1)} %up_hbm.1, ...), custom_call_target="tpu_custom_call" | custom-call | tf_op jit(solution)/shard_map/cross_layer/pallas_call | solution.py:510
  47.5 0.9 %finish.1 = (bf16[128,128]{1,0:T(8,128)(2,1)}, bf16[128,128]{1,0:T(8,128)(2,1)}, bf16[128,128]{1,0:T(8,128)(2,1)}, f32[4,2,128,128]{3,2,1,0:T(8,128)}, f32[1,128]{1,0:T(1,128)}) custom-call(bf16[128,128]{1,0:T(8,128)(2,1)S(1)} %get-tuple-element.15.a, bf16[128,128]{1,0:T(8,128)(2,1)S(1)} %get-tuple-element.16.b, bf16[128,128]{1,0:T(8,128)(2,1)S(1)} %get-tuple-element.17.e, ...), custom_call_target="tpu_custom_call" | custom-call | tf_op jit(solution)/shard_map/finish/pallas_call | solution.py:564

commit v4 on v3

--- a/solution.py
+++ b/solution.py
@@ -12,7 +12,7 @@
 F32 = jnp.float32
 BF16 = jnp.bfloat16
 N_SENDS = 14
-N_RECVS = 49
+N_RECVS = 50
 MOST_ROWS = 4096
 
 
@@ -37,6 +37,7 @@
     dl,
     dlp,
     xa,
+    fs,
     xb,
     do,
     dp_,
@@ -111,7 +112,6 @@
         wait_rows(recv.at[k], sum(rows(ref) for ref in landed))
 
     b4, b2, b1 = lax.div(d, 4), lax.rem(lax.div(d, 2), 2), lax.rem(d, 2)
-    mine = d == 2 * x + h
 
     def first_row(d_, h_):
         window = jnp.clip(d_ - 2, 0, 4)
@@ -121,25 +121,12 @@
     near = [dev(c_=oc)]
     near += [dev(x_=plus(x, k)) for k in (1, 2, 3)]
     near += [dev(y_=plus(y, k)) for k in (1, 2, 3)]
-    near += [dev(h_=oh), dev(d_=d + 4 - 8 * b4), dev(d_=d + 2 - 4 * b2), dev(d_=d + 1 - 2 * b1)]
+    z = h * 8 + d
+    for k in range(1, 16):
+        zk = lax.rem(z + k, 16)
+        near.append(dev(h_=lax.div(zk, 8), d_=lax.rem(zk, 8)))
     for to in near:
         pl.semaphore_signal(barrier, inc=1, device_id=to, device_id_type=MESH)
-    z_to = []
-    for t in range(4):
-        for hh in (0, 1):
-            same = jnp.logical_and(x == t, jnp.logical_and(h == hh, mine))
-            z_to.append((t, hh, same, dev(x_=t, h_=hh, d_=2 * x + h)))
-    z_from = []
-    for s in range(8):
-        same = jnp.logical_and(d == s, mine)
-        z_from.append((same, dev(x_=lax.div(d, 2), h_=lax.rem(d, 2), d_=s)))
-    for same, to in [(same, to) for _, _, same, to in z_to] + z_from:
-
-        @pl.when(jnp.logical_not(same))
-        def _(to=to):
-            pl.semaphore_signal(barrier, inc=1, device_id=to, device_id_type=MESH)
-
-    n_signals = len(near) + 16 - 2 * mine.astype(jnp.int32)
 
     loads = [
         pltpu.make_async_copy(src, dst, lsem.at[k])
@@ -157,31 +144,33 @@
     for load in loads:
         load.start()
     loads[0].wait()
-    pl.semaphore_wait(barrier, n_signals)
+    pl.semaphore_wait(barrier, len(near))
 
     def ag1(view, n):
         half = n // 2
+        a = view(x, y, 0, half)
+        b = view(x, y, half, half)
         k = next(ids)
         for j in (1, 3, 2):
-            a = view(x, y, 0, half)
-            b = view(x, y, half, half)
             put(a, a, dev(x_=plus(x, j)), k)
             put(b, b, dev(y_=plus(y, j)), k)
-        return k
-
-    def ag1_wait(view, n, k):
-        half = n // 2
-        got(k, *[view(x, y, 0, half)] * 3, *[view(x, y, half, half)] * 3)
-
-    every = pl.ds(0, 4)
-
-    def ag2(view, n):
-        half = n // 2
         ks = []
         for j in (1, 3):
-            a = view(every, y, 0, half)
-            b = view(x, every, half, half)
             ks.append((put(a, a, dev(y_=plus(y, j))), put(b, b, dev(x_=plus(x, j)))))
+        return k, ks
+
+    every = pl.ds(0, 4)
+
+    def ag2(view, n, sent1):
+        half = n // 2
+        k, ks = sent1
+        got(k, *[view(x, y, 0, half)] * 3, *[view(x, y, half, half)] * 3)
+        for (ka, kb), j in zip(ks, (1, 3), strict=True):
+            for i in (1, 3, 2):
+                a = view(plus(x, i), y, 0, half)
+                b = view(x, plus(y, i), half, half)
+                put(a, a, dev(y_=plus(y, j)), ka)
+                put(b, b, dev(x_=plus(x, j)), kb)
         return ks
 
     def ag2_forward(view, n, ks):
@@ -213,35 +202,47 @@
     def x_block1(xs, ys, q, nq):
         return xb.at[xs, ys, pl.ds(4 + q, nq)]
 
+    k_zx = put(lay, xa.at[h, x, y], dev(h_=oh))
+    k_fs = next(ids)
+    for j in (2, 1, 3):
+        t = plus(x, j)
+        put(lay.at[t], fs.at[x], dev(x_=t), k_fs)
     z_first = [next(send_ids) for _ in range(8)]
     z_recv = next(ids)
     next(ids)
     z_sent = []
-    for n, (t, hh, same, to) in enumerate(z_to):
-        d_to = 2 * x + h
-        slot = lax.rem(d + 8 - first_row(d_to, hh), 8)
-        src, dst = lay.at[t], xb.at[t, y, slot]
-        copy = pltpu.make_async_remote_copy(
-            src_ref=src,
-            dst_ref=dst,
-            send_sem=send.at[z_first[n]],
-            recv_sem=recv.at[z_recv + lax.div(slot, 4)],
-            device_id=to,
-            device_id_type=MESH,
-        )
-        stay = pltpu.make_async_copy(src, dst, recv.at[z_recv + lax.div(slot, 4)])
-
-        @pl.when(same)
-        def _(stay=stay):
-            stay.start()
-
-        @pl.when(jnp.logical_not(same))
-        def _(copy=copy):
-            copy.start()
-
-        z_sent.append((same, copy))
-
-    k_zx = put(lay, xa.at[h, x, y], dev(h_=oh))
+
+    def along_z_to_block(j):
+        s = plus(x, j)
+        src = lay.at[x] if j == 0 else fs.at[s]
+        d_to = 2 * s + h
+        for hh in (0, 1):
+            n = 2 * j + hh
+            same = jnp.logical_and(h == hh, d_to == d)
+            slot = lax.rem(d + 8 - first_row(d_to, hh), 8)
+            dst = xb.at[x, y, slot]
+            copy = pltpu.make_async_remote_copy(
+                src_ref=src,
+                dst_ref=dst,
+                send_sem=send.at[z_first[n]],
+                recv_sem=recv.at[z_recv + lax.div(slot, 4)],
+                device_id=dev(h_=hh, d_=d_to),
+                device_id_type=MESH,
+            )
+            stay = pltpu.make_async_copy(src, dst, recv.at[z_recv + lax.div(slot, 4)])
+
+            @pl.when(same)
+            def _(stay=stay):
+                stay.start()
+
+            @pl.when(jnp.logical_not(same))
+            def _(copy=copy):
+                copy.start()
+
+            z_sent.append((same, copy))
+
+    along_z_to_block(0)
+
     k_wp = [put(w4.at[:, oh, :, oc], wp.at[:, oh], dev(c_=oc))]
     loads[3].wait()
     own1 = ag1(x_own, 4)
@@ -256,7 +257,6 @@
     do[:, b4, b2, b1] = low
     bs[b4, b2, b1] = jnp.broadcast_to(jnp.sum(delta, axis=0, keepdims=True), (8, 128))
     k_dlp = put(dl, dlp, dev(c_=oc))
-    k_wp.append(put(w4.at[:, h, :, oc], wp.at[:, h], dev(c_=oc)))
 
     every2 = pl.ds(0, 2)
     steps = (
@@ -275,6 +275,7 @@
         got(k, do.at[(slice(None), *theirs)], bs.at[theirs])
 
     k_d = along_z(0)
+    k_wp.append(put(w4.at[:, h, :, oc], wp.at[:, h], dev(c_=oc)))
 
     loads[5].wait()
     got(k_dlp, dlp)
@@ -368,10 +369,12 @@
     back_terms(h)
     k_near = rs1(h)
 
-    ag1_wait(x_own, 4, own1)
-    own2 = ag2(x_own, 4)
+    got(k_fs, lay.at[pl.ds(0, 3)])
+    for j in (1, 2, 3):
+        along_z_to_block(j)
     k_far = rs2(oh, k_far)
     k_near = rs2(h, k_near)
+    own2 = ag2(x_own, 4, own1)
 
     def mixed_terms(hs, acc):
         for xs in range(4):
@@ -383,31 +386,28 @@
         return acc
 
     quarter = xb.at[x, y, pl.ds(0, 4)]
+    got(k_zx, xa.at[oh, x, y])
+    other1 = ag1(x_other, 4)
     got(z_recv, quarter)
     first1 = ag1(x_block0, 4)
-    got(k_zx, xa.at[oh, x, y])
-    other1 = ag1(x_other, 4)
     k_far = rs3(oh, k_far)
+    along_z_wait(0, k_d)
+    k_d = along_z(1)
     got(z_recv + 1, quarter)
     second1 = ag1(x_block1, 4)
     k_near = rs3(h, k_near)
 
-    along_z_wait(0, k_d)
-    k_d = along_z(1)
     own3 = ag2_forward(x_own, 4, own2)
-    ag1_wait(x_block0, 4, first1)
-    first2 = ag2(x_block0, 4)
-    ag1_wait(x_other, 4, other1)
-    other2 = ag2(x_other, 4)
+    first2 = ag2(x_block0, 4, first1)
+    other2 = ag2(x_other, 4, other1)
+    along_z_wait(1, k_d)
+    k_d = along_z(2)
 
     rs4(oh, k_far)
     zs[...] = tt[oh].astype(BF16)
     k_zr = put(zs, zr, dev(h_=oh))
 
-    ag1_wait(x_block1, 4, second1)
-    second2 = ag2(x_block1, 4)
-    along_z_wait(1, k_d)
-    k_d = along_z(2)
+    second2 = ag2(x_block1, 4, second1)
     ag2_wait(x_own, 4, own3)
     mixp[...] = mixed_terms(h, jnp.zeros((128, 256), F32))
 
@@ -431,7 +431,7 @@
             out.append(ref[xs, lax.div(s, 4), lax.rem(lax.div(s, 2), 2), lax.rem(s, 2)])
         return jnp.concatenate(out, axis=0)
 
-    def weight_terms(g):
+    def weight_terms(g, ref):
         feats = jnp.concatenate(
             [
                 jnp.concatenate(
@@ -441,26 +441,18 @@
             ],
             axis=0,
         )
-        cols = jnp.concatenate(
-            [
-                jnp.concatenate(
-                    [rows_of(do, xs, g), rows_of(dp_, xs, g)], axis=1
-                )
-                for xs in range(4)
-            ],
-            axis=0,
-        )
+        cols = jnp.concatenate([rows_of(ref, xs, g) for xs in range(4)], axis=0)
         return lax.dot_general(feats, cols, tn, preferred_element_type=F32)
 
     got(k_dp, dp_)
     ag2_wait(x_block0, 4, first3)
-    acc = weight_terms(0)
+    theirs, ours = weight_terms(0, dp_), weight_terms(0, do)
     ag2_wait(x_block1, 4, second3)
-    acc = acc + weight_terms(1)
-    acc = acc * scale
-    gws[...] = acc[:, 128:256].reshape(4, 128, 128)
+    theirs = theirs + weight_terms(1, dp_)
+    gws[...] = (theirs * scale).reshape(4, 128, 128)
     k_gw = put(gws, gw.at[:, c], dev(c_=oc))
-    gw[:, c] = acc[:, 0:128].reshape(4, 128, 128)
+    ours = ours + weight_terms(1, do)
+    gw[:, c] = (ours * scale).reshape(4, 128, 128)
 
     gbias[...] = jnp.sum(bs[...].reshape(8, 8, 128)[:, 0], axis=0, keepdims=True) * scale
 
@@ -522,6 +514,7 @@
             pltpu.VMEM((4, 32, 128), BF16),
             pltpu.VMEM((4, 32, 128), BF16),
             pltpu.VMEM((2, 4, 4, 4, 32, 128), BF16),
+            pltpu.VMEM((4, 32, 128), BF16),
             pltpu.VMEM((4, 4, 8, 32, 128), BF16),
             pltpu.VMEM((4, 2, 2, 2, 32, 128), BF16),
             pltpu.VMEM((4, 2, 2, 2, 32, 128), BF16),

time: 48.5 us -> 45.5 us (0.938)
  Pallas kernels: 47.8 us -> 44.8 us
    pallas_call x1, Pallas kernels: 46.9 us -> 43.9 us  [local(): pl.pallas_call(functools.partial(kernel, scale), out_shape=shapes, in_spe...]
where the time goes in v4:
time: 45.5 us; the launch traced here: 45.4 us
  Pallas kernels  44.8 us (98%)
  between operations  0.64 us (1%)
    pallas_call x1, Pallas kernels, local(): pl.pallas_call(functools.partial(kernel, scale), out_shape=shapes, in_spe...  43.9 us

profile of v4, /device:TPU:1, one launch (start us, length us, event | category | flops | bytes accessed | tf_op | source)
XLA Modules:
  0.0 45.4 jit_solution(9146324434279138987)
XLA Ops:
  0.6 43.9 %cross_layer.1 = (bf16[128,128]{1,0:T(8,128)(2,1)S(1)}, bf16[128,128]{1,0:T(8,128)(2,1)S(1)}, bf16[128,128]{1,0:T(8,128)(2,1)S(1)}, f32[4,2,128,128]{3,2,1,0:T(8,128)S(1)}, f32[1,128]{1,0:T(1,128)S(1)}) custom-call(bf16[128,128]{1,0:T(8,128)(2,1)} %base_hbm.1, bf16[4,32,128]{2,1,0:T(8,128)(2,1)} %bitcast.6, bf16[128,128]{1,0:T(8,128)(2,1)} %up_hbm.1, ...), custom_call_target="tpu_custom_call" | custom-call | tf_op jit(solution)/shard_map/cross_layer/pallas_call | solution.py:502
  44.5 0.9 %finish.1 = (bf16[128,128]{1,0:T(8,128)(2,1)}, bf16[128,128]{1,0:T(8,128)(2,1)}, bf16[128,128]{1,0:T(8,128)(2,1)}, f32[4,2,128,128]{3,2,1,0:T(8,128)}, f32[1,128]{1,0:T(1,128)}) custom-call(bf16[128,128]{1,0:T(8,128)(2,1)S(1)} %get-tuple-element.15.a, bf16[128,128]{1,0:T(8,128)(2,1)S(1)} %get-tuple-element.16.b, bf16[128,128]{1,0:T(8,128)(2,1)S(1)} %get-tuple-element.17.e, ...), custom_call_target="tpu_custom_call" | custom-call | tf_op jit(solution)/shard_map/finish/pallas_call | solution.py:557

commit v5 on v4

--- a/solution.py
+++ b/solution.py
@@ -118,13 +118,14 @@
         return jnp.where(lax.rem(d_, 2) == h_, window, window + 4)
 
     barrier = pltpu.get_barrier_semaphore()
-    near = [dev(c_=oc)]
-    near += [dev(x_=plus(x, k)) for k in (1, 2, 3)]
-    near += [dev(y_=plus(y, k)) for k in (1, 2, 3)]
+    near = []
     z = h * 8 + d
-    for k in range(1, 16):
+    for k in (8, 7, 9, 6, 10, 5, 11, 4, 12, 3, 13, 2, 14, 1, 15):
         zk = lax.rem(z + k, 16)
         near.append(dev(h_=lax.div(zk, 8), d_=lax.rem(zk, 8)))
+    near += [dev(x_=plus(x, k)) for k in (2, 1, 3)]
+    near += [dev(y_=plus(y, k)) for k in (2, 1, 3)]
+    near.append(dev(c_=oc))
     for to in near:
         pl.semaphore_signal(barrier, inc=1, device_id=to, device_id_type=MESH)
 
@@ -372,9 +373,9 @@
     got(k_fs, lay.at[pl.ds(0, 3)])
     for j in (1, 2, 3):
         along_z_to_block(j)
+    own2 = ag2(x_own, 4, own1)
     k_far = rs2(oh, k_far)
     k_near = rs2(h, k_near)
-    own2 = ag2(x_own, 4, own1)
 
     def mixed_terms(hs, acc):
         for xs in range(4):
@@ -390,6 +391,7 @@
     other1 = ag1(x_other, 4)
     got(z_recv, quarter)
     first1 = ag1(x_block0, 4)
+    own3 = ag2_forward(x_own, 4, own2)
     k_far = rs3(oh, k_far)
     along_z_wait(0, k_d)
     k_d = along_z(1)
@@ -397,7 +399,6 @@
     second1 = ag1(x_block1, 4)
     k_near = rs3(h, k_near)
 
-    own3 = ag2_forward(x_own, 4, own2)
     first2 = ag2(x_block0, 4, first1)
     other2 = ag2(x_other, 4, other1)
     along_z_wait(1, k_d)
@@ -422,7 +423,6 @@
     mixp[...] = mixed_terms(oh, mixp[...])
     k_mix = put(mixp.at[:, pl.ds(128, 128)], mixr, dev(c_=oc))
 
-    tn = (((0,), (0,)), ((), ()))
 
     def rows_of(ref, xs, g):
         out = []
@@ -431,28 +431,31 @@
             out.append(ref[xs, lax.div(s, 4), lax.rem(lax.div(s, 2), 2), lax.rem(s, 2)])
         return jnp.concatenate(out, axis=0)
 
-    def weight_terms(g, ref):
-        feats = jnp.concatenate(
+    def features(g):
+        return jnp.concatenate(
             [
                 jnp.concatenate(
                     [xb[xs, ys, 4 * g : 4 * g + 4].reshape(128, 128) for ys in range(4)], axis=1
-                )
+                ).T
                 for xs in range(4)
             ],
-            axis=0,
+            axis=1,
         )
+
+    def weight_terms(feats, g, ref):
         cols = jnp.concatenate([rows_of(ref, xs, g) for xs in range(4)], axis=0)
-        return lax.dot_general(feats, cols, tn, preferred_element_type=F32)
+        return jnp.dot(feats, cols, preferred_element_type=F32)
 
     got(k_dp, dp_)
     ag2_wait(x_block0, 4, first3)
-    theirs, ours = weight_terms(0, dp_), weight_terms(0, do)
+    feats = features(0)
+    gws[...] = weight_terms(feats, 0, dp_).reshape(4, 128, 128)
+    gw[:, c] = weight_terms(feats, 0, do).reshape(4, 128, 128)
     ag2_wait(x_block1, 4, second3)
-    theirs = theirs + weight_terms(1, dp_)
-    gws[...] = (theirs * scale).reshape(4, 128, 128)
+    feats = features(1)
+    gws[...] = (gws[...] + weight_terms(feats, 1, dp_).reshape(4, 128, 128)) * scale
     k_gw = put(gws, gw.at[:, c], dev(c_=oc))
-    ours = ours + weight_terms(1, do)
-    gw[:, c] = (ours * scale).reshape(4, 128, 128)
+    gw[:, c] = (gw[:, c] + weight_terms(feats, 1, do).reshape(4, 128, 128)) * scale
 
     gbias[...] = jnp.sum(bs[...].reshape(8, 8, 128)[:, 0], axis=0, keepdims=True) * scale
 
@@ -479,7 +482,18 @@
 def finish(a, b, e, g, s, oa, ob, oe, og, os_, sem):
     copies = [
         pltpu.make_async_copy(src, dst, sem.at[k])
-        for k, (src, dst) in enumerate(((g, og), (a, oa), (b, ob), (e, oe), (s, os_)))
+        for k, (src, dst) in enumerate(
+            (
+                (g.at[0], og.at[0]),
+                (g.at[1], og.at[1]),
+                (g.at[2], og.at[2]),
+                (g.at[3], og.at[3]),
+                (a, oa),
+                (b, ob),
+                (e, oe),
+                (s, os_),
+            )
+        )
     ]
     for copy in copies:
         copy.start()
@@ -559,7 +573,7 @@
         out_shape=shapes,
         in_specs=[vmem] * 5,
         out_specs=(pl.BlockSpec(memory_space=pl.ANY),) * 5,
-        scratch_shapes=[pltpu.SemaphoreType.DMA((5,))],
+        scratch_shapes=[pltpu.SemaphoreType.DMA((8,))],
         compiler_params=pltpu.CompilerParams(vmem_limit_bytes=4 << 20),
         name="finish",
     )(*results)

time: 45.5 us -> 45.1 us (level)
  Pallas kernels: 44.8 us -> 44.3 us
where the time goes in v5:
time: 45.1 us; the launch traced here: 45 us
  Pallas kernels  44.3 us (98%)
  between operations  0.64 us (1%)
    pallas_call x1, Pallas kernels, local(): pl.pallas_call(functools.partial(kernel, scale), out_shape=shapes, in_spe...  43.5 us

profile of v5, /device:TPU:1, one launch (start us, length us, event | category | flops | bytes accessed | tf_op | source)
XLA Modules:
  0.0 45.0 jit_solution(2066605606153169908)
XLA Ops:
  0.6 43.5 %cross_layer.1 = (bf16[128,128]{1,0:T(8,128)(2,1)S(1)}, bf16[128,128]{1,0:T(8,128)(2,1)S(1)}, bf16[128,128]{1,0:T(8,128)(2,1)S(1)}, f32[4,2,128,128]{3,2,1,0:T(8,128)S(1)}, f32[1,128]{1,0:T(1,128)S(1)}) custom-call(bf16[128,128]{1,0:T(8,128)(2,1)} %base_hbm.1, bf16[4,32,128]{2,1,0:T(8,128)(2,1)} %bitcast.6, bf16[128,128]{1,0:T(8,128)(2,1)} %up_hbm.1, ...), custom_call_target="tpu_custom_call" | custom-call | tf_op jit(solution)/shard_map/cross_layer/pallas_call | solution.py:516
  44.1 0.9 %finish.1 = (bf16[128,128]{1,0:T(8,128)(2,1)}, bf16[128,128]{1,0:T(8,128)(2,1)}, bf16[128,128]{1,0:T(8,128)(2,1)}, f32[4,2,128,128]{3,2,1,0:T(8,128)}, f32[1,128]{1,0:T(1,128)}) custom-call(bf16[128,128]{1,0:T(8,128)(2,1)S(1)} %get-tuple-element.15.a, bf16[128,128]{1,0:T(8,128)(2,1)S(1)} %get-tuple-element.16.b, bf16[128,128]{1,0:T(8,128)(2,1)S(1)} %get-tuple-element.17.e, ...), custom_call_target="tpu_custom_call" | custom-call | tf_op jit(solution)/shard_map/finish/pallas_call | solution.py:571

commit v6 on v5

--- a/solution.py
+++ b/solution.py
@@ -387,10 +387,10 @@
         return acc
 
     quarter = xb.at[x, y, pl.ds(0, 4)]
+    got(z_recv, quarter)
+    first1 = ag1(x_block0, 4)
     got(k_zx, xa.at[oh, x, y])
     other1 = ag1(x_other, 4)
-    got(z_recv, quarter)
-    first1 = ag1(x_block0, 4)
     own3 = ag2_forward(x_own, 4, own2)
     k_far = rs3(oh, k_far)
     along_z_wait(0, k_d)

time: 45.1 us -> 44.9 us (level)
  no operation moved by 1% of the time
where the time goes in v6:
time: 44.9 us; the launch traced here: 44.8 us
  Pallas kernels  44.2 us (98%)
  between operations  0.64 us (1%)
    pallas_call x1, Pallas kernels, local(): pl.pallas_call(functools.partial(kernel, scale), out_shape=shapes, in_spe...  43.3 us

profile of v6, /device:TPU:1, one launch (start us, length us, event | category | flops | bytes accessed | tf_op | source)
XLA Modules:
  0.0 44.8 jit_solution(8530297825028416299)
XLA Ops:
  0.6 43.3 %cross_layer.1 = (bf16[128,128]{1,0:T(8,128)(2,1)S(1)}, bf16[128,128]{1,0:T(8,128)(2,1)S(1)}, bf16[128,128]{1,0:T(8,128)(2,1)S(1)}, f32[4,2,128,128]{3,2,1,0:T(8,128)S(1)}, f32[1,128]{1,0:T(1,128)S(1)}) custom-call(bf16[128,128]{1,0:T(8,128)(2,1)} %base_hbm.1, bf16[4,32,128]{2,1,0:T(8,128)(2,1)} %bitcast.6, bf16[128,128]{1,0:T(8,128)(2,1)} %up_hbm.1, ...), custom_call_target="tpu_custom_call" | custom-call | tf_op jit(solution)/shard_map/cross_layer/pallas_call | solution.py:516
  43.9 0.9 %finish.1 = (bf16[128,128]{1,0:T(8,128)(2,1)}, bf16[128,128]{1,0:T(8,128)(2,1)}, bf16[128,128]{1,0:T(8,128)(2,1)}, f32[4,2,128,128]{3,2,1,0:T(8,128)}, f32[1,128]{1,0:T(1,128)}) custom-call(bf16[128,128]{1,0:T(8,128)(2,1)S(1)} %get-tuple-element.15.a, bf16[128,128]{1,0:T(8,128)(2,1)S(1)} %get-tuple-element.16.b, bf16[128,128]{1,0:T(8,128)(2,1)S(1)} %get-tuple-element.17.e, ...), custom_call_target="tpu_custom_call" | custom-call | tf_op jit(solution)/shard_map/finish/pallas_call | solution.py:571
